TPU v7x, 512 devices: a whole 4x4x16 slice. The times are simulated.
512 devices in a mesh: loop: 32 (over z, y_hi), rep: 4 (over x), feat: 4 (over y_lo, core).
Axes of the slice: x: 4, y: 4 (y_hi: 2, y_lo: 2; y = y_hi * 2 + y_lo), z: 16, core: 2. Of those that a mesh axis runs over, the one named last changes fastest.
Arguments:
- features: bfloat16 [128, 32768], P('feat', 'loop'), may hold values from -6 to 6
- tile_values: bfloat16 [32, 4, 112, 128, 128], P('loop', 'rep'), may hold values from -0.1875 to 0.1875
- tile_coords: int32 [32, 4, 2, 112], P('loop', 'rep'), may hold values from 0 to 7, as said below
- section_counts: int32 [32, 4, 8], P('loop', 'rep'), may hold values from 0 to 64, as said below
- weight_one: bfloat16 [128, 128], replicated, may hold values from -0.5 to 0.5
- weight_two: bfloat16 [128, 128], replicated, may hold values from -0.5 to 0.5
- cotangent: bfloat16 [128, 32768], P(None, ('loop', 'feat')), may hold values from -24 to 24
Outputs:
- grad_one: float32 [128, 128], replicated
- grad_two: float32 [128, 128], replicated
- input_grad: bfloat16 [128, 32768], P('feat', 'loop')
Inputs may be any that keep to these rules, and one draw needn't show every extreme that they name: `tile_coords`: slots of a list are grouped by section in order of sections; the live slots of one section name distinct (row, column) pairs; slots past the list's total count hold 0. `section_counts`: section k of rep index r covers the column block r + 4 * k places below the list's own loop index; sections with r + 4 * k of 32 or more hold 0.
All inputs are finite; a program needn't handle non-finite values.
Results may differ from a plain program's by a relative error of at most 0.029.
Values may be sent and summed in bfloat16 or wider, within the bound.
A program may use at most 64 MiB of HBM per device.

v0:
```python
import math
import jax
import jax.numpy as jnp
from jax import lax
from jax.sharding import PartitionSpec as P

tile_batch = 8


def passed_along(value, axis, steps):
    count = lax.axis_size(axis)
    pairs = [(source, (source + steps) % count) for source in range(count)]
    return lax.ppermute(value, axis, pairs)


def silu_slope(argument):
    sigmoid_value = jax.nn.sigmoid(argument)
    return sigmoid_value * (1.0 + argument * (1.0 - sigmoid_value))


def section_term(source, section_id, layout, transposed, enabled=True):
    tile_set, row_ids, col_ids, starts, filled, panels = layout
    feat_width = source.shape[0]
    tile_side = tile_set.shape[-1]
    slot_total = tile_set.shape[0]
    shaped = source.reshape(feat_width, panels, tile_side)
    first = starts[section_id]
    number = jnp.where(enabled, filled[section_id], 0)
    rounds = (number + tile_batch - 1) // tile_batch
    offsets = jnp.arange(tile_batch, dtype=jnp.int32)
    panel_ids = jnp.arange(panels, dtype=jnp.int32)

    def one_round(round_id, running):
        within = round_id * tile_batch + offsets
        alive_mask = within < number
        slot_ids = jnp.minimum(first + within, slot_total - 1)
        chosen = tile_set[slot_ids]
        if transposed:
            picked = shaped[:, row_ids[slot_ids], :]
            products = jnp.einsum(
                "dba,bac->dbc", picked, chosen, preferred_element_type=jnp.float32
            )
            target = col_ids[slot_ids]
        else:
            picked = shaped[:, col_ids[slot_ids], :]
            products = jnp.einsum(
                "dbc,bac->dba", picked, chosen, preferred_element_type=jnp.float32
            )
            target = row_ids[slot_ids]
        placing = ((target[:, None] == panel_ids[None, :]) & alive_mask[:, None]).astype(
            jnp.float32
        )
        return running + jnp.einsum(
            "dbe,bp->dpe", products, placing, precision=lax.Precision.HIGHEST
        )

    zero_block = jnp.zeros((feat_width, panels, tile_side), jnp.float32)
    return lax.fori_loop(0, rounds, one_round, zero_block).reshape(feat_width, panels * tile_side)


def advance(block, stride):
    return passed_along(block, "loop", stride)


def forward_product(source, layout):
    loop_size = lax.axis_size("loop")
    rep_size = lax.axis_size("rep")
    rep_index = lax.axis_index("rep")
    sections = -(-loop_size // rep_size)
    stride = rep_size % loop_size
    current = source
    for bit in range(rep_size.bit_length() - 1):
        jump = (1 << bit) % loop_size
        moved = passed_along(current, "loop", jump)
        current = jnp.where((rep_index >> bit) % 2 == 1, moved, current)
    running = section_term(current, 0, layout, False)

    def onward(step_id, carry):
        ahead, acc = carry
        ahead = advance(ahead, stride)
        return (ahead, acc + section_term(ahead, step_id, layout, False))

    ahead, running = lax.fori_loop(1, sections, onward, (current, running))
    return running


def transposed_product(source, layout):
    loop_size = lax.axis_size("loop")
    rep_size = lax.axis_size("rep")
    rep_index = lax.axis_index("rep")
    sections = -(-loop_size // rep_size)
    stride = rep_size % loop_size
    running = section_term(source, sections - 1, layout, True)

    def backward(step_id, acc):
        acc = passed_along(acc.astype(jnp.bfloat16), "loop", -stride).astype(acc.dtype)
        return acc + section_term(source, sections - 1 - step_id, layout, True)

    running = lax.fori_loop(1, sections, backward, running)
    for bit in range(rep_size.bit_length() - 1):
        jump = (1 << bit) % loop_size
        moved = passed_along(running.astype(jnp.bfloat16), "loop", -jump).astype(running.dtype)
        running = jnp.where((rep_index >> bit) % 2 == 1, moved, running)
    return running


def to_nodes(partial_value):
    summed = lax.psum(partial_value.astype(jnp.bfloat16), "rep")
    return lax.all_to_all(summed, "feat", split_axis=1, concat_axis=0, tiled=True)


def to_features(node_block):
    return lax.all_to_all(node_block, "feat", split_axis=0, concat_axis=1, tiled=True)


def weight_grad(mixed, slope):
    part_sum = jnp.einsum("dq,eq->de", mixed, slope, preferred_element_type=jnp.float32)
    return lax.psum(part_sum, ("loop", "feat"))


def shards(features, tile_values, tile_coords, section_counts, weight_one, weight_two, cotangent):
    tile_set = tile_values[0, 0]
    row_ids = tile_coords[0, 0, 0]
    col_ids = tile_coords[0, 0, 1]
    filled = section_counts[0, 0]
    starts = jnp.cumsum(filled) - filled
    panels = features.shape[1] // tile_set.shape[-1]
    layout = (tile_set, row_ids, col_ids, starts, filled, panels)
    scale = 1.0 / math.sqrt(features.shape[1] * lax.axis_size("loop"))
    mix_one = to_nodes(forward_product(features, layout))
    z_one = jnp.einsum("de,dq->eq", weight_one, mix_one, preferred_element_type=jnp.float32)
    h_one = jax.nn.silu(z_one).astype(jnp.bfloat16)
    mix_two = to_nodes(forward_product(to_features(h_one), layout))
    z_two = jnp.einsum("de,dq->eq", weight_two, mix_two, preferred_element_type=jnp.float32)
    dz_two = (cotangent * silu_slope(z_two)).astype(jnp.bfloat16)
    grad_two = weight_grad(mix_two, dz_two) * scale
    dm_two = jnp.einsum("de,eq->dq", weight_two, dz_two, preferred_element_type=jnp.float32).astype(
        jnp.bfloat16
    )
    dh_one = to_nodes(transposed_product(to_features(dm_two), layout))
    dz_one = (dh_one * silu_slope(z_one)).astype(jnp.bfloat16)
    grad_one = weight_grad(mix_one, dz_one) * scale
    dm_one = jnp.einsum("de,eq->dq", weight_one, dz_one, preferred_element_type=jnp.float32).astype(
        jnp.bfloat16
    )
    partial_value = transposed_product(to_features(dm_one), layout)
    input_grad = lax.psum(partial_value.astype(jnp.bfloat16), "rep")
    return (grad_one, grad_two, input_grad)


def solution(mesh):
    return jax.shard_map(
        shards,
        mesh=mesh,
        in_specs=(
            P("feat", "loop"),
            P("loop", "rep", None, None, None),
            P("loop", "rep", None, None),
            P("loop", "rep", None),
            P(),
            P(),
            P(None, ("loop", "feat")),
        ),
        out_specs=(P(), P(), P("feat", "loop")),
        check_vma=False,
    )
```

profile of v0, /device:TPU:8, one launch (start us, length us, event | category | flops | bytes accessed | tf_op | source)
XLA Modules:
  0.0 1272.7 jit_solution(16373129460673330023)
XLA Ops:
  15.7 7.1 collective-permute-done.4
  31.1 51.0 %while.294 = (s32[]{:T(128)}, f32[32,8,128]{2,1,0:T(8,128)S(1)}, s32[]{:T(128)}, s32[]{:T(128)}, s32[112]{0:T(128)S(1)}, /*index=5*/s32[]{:T(128)}, bf16[112,128...) while((s32[]{:T(128)}, f32[32,8,128]{2,1,0:T(8,128)S(1)}, ...), condition=%wide.region_2.3_spmd.clone.clone, body=%wide.region_1.2_spmd.clone.clone.sunk | while | flops 11569371 | bytes 1516121 | solution.py:58
  82.2 106.4 %while.287 = (s32[]{:T(128)}, bf16[32,1024]{1,0:T(8,128)(2,1)S(1)}, f32[32,1024]{1,0:T(8,128)S(1)}, s32[8]{0:T(128)S(1)}, s32[8]{0:T(128)S(1)}, /*index=5*/s32[1...) while((s32[]{:T(128)}, bf16[32,1024]{1,0:T(8,128)(2,1)S(1)}, ...), condition=%wide.region_6.7_spmd, body=%wide.region_3.6_spmd.sunk | while | flops 11602160 | bytes 2565222 | solution.py:83
  90.9 12.7 while.298
  142.5 6.9 collective-permute-start.3
  189.4 54.5 %all-reduce.7.cloned.1.call-done = bf16[32,4,256]{2,1,0:T(4,128)(2,1)} async-done(((bf16[32,4,256]{2,1,0:T(4,128)(2,1)}), bf16[32,4,256]{2,1,0:T(4,128)(2,1)}) %all-reduce.7.cloned.1.call-update) | async-done | bytes 65552 | tf_op jit(solution)/shard_map/psum | solution.py:108
  274.0 51.0 %while.295 = (s32[]{:T(128)}, f32[32,8,128]{2,1,0:T(8,128)S(1)}, s32[]{:T(128)}, s32[]{:T(128)}, s32[112]{0:T(128)S(1)}, /*index=5*/s32[]{:T(128)}, bf16[112,128...) while((s32[]{:T(128)}, f32[32,8,128]{2,1,0:T(8,128)S(1)}, ...), condition=%wide.region_9.10_spmd.clone.clone, body=%wide.region_8.9_spmd.clone.clone.sunk | while | flops 11569371 | bytes 1516121 | solution.py:58
  325.1 106.4 %while.289 = (s32[]{:T(128)}, bf16[32,1024]{1,0:T(8,128)(2,1)S(1)}, f32[32,1024]{1,0:T(8,128)S(1)}, s32[8]{0:T(128)S(1)}, s32[8]{0:T(128)S(1)}, /*index=5*/s32[1...) while((s32[]{:T(128)}, bf16[32,1024]{1,0:T(8,128)(2,1)S(1)}, ...), condition=%wide.region_13.14_spmd, body=%wide.region_10.13_spmd.sunk | while | flops 11602160 | bytes 2565222 | solution.py:83
  334.0 12.7 while.299
  385.4 7.0 collective-permute-start.2
  432.2 57.9 %all-reduce.9.cloned.1.call-done = bf16[32,4,256]{2,1,0:T(4,128)(2,1)} async-done(((bf16[32,4,256]{2,1,0:T(4,128)(2,1)}), bf16[32,4,256]{2,1,0:T(4,128)(2,1)}) %all-reduce.9.cloned.1.call-update) | async-done | bytes 65552 | tf_op jit(solution)/shard_map/psum | solution.py:108
  511.3 135.5 %while.291 = (s32[]{:T(128)}, bf16[32,1024]{1,0:T(8,128)(2,1)S(1)}, s32[8]{0:T(128)S(1)}, s32[8]{0:T(128)S(1)}, bf16[32,1024]{1,0:T(8,128)(2,1)S(1)}, /*index=5*...) while((s32[]{:T(128)}, bf16[32,1024]{1,0:T(8,128)(2,1)S(1)}, ...), condition=%wide.region_20.21_spmd, body=%wide.region_17.20_spmd.sunk | while | flops 11667697 | bytes 2303082 | solution.py:99
  526.4 10.4 collective-permute-start.1
  579.8 12.6 while.300
  596.4 50.3 %while.300 = (s32[]{:T(128)}, f32[32,8,128]{2,1,0:T(8,128)S(1)}, s32[]{:T(128)}, s32[]{:T(128)}, s32[112]{0:T(128)S(1)}, /*index=5*/s32[]{:T(128)}, bf16[112,128...) while((s32[]{:T(128)}, f32[32,8,128]{2,1,0:T(8,128)S(1)}, ...), condition=%wide.region_19.19_spmd.clone.clone, body=%wide.region_18.18_spmd.clone.clone.sunk | while | flops 11569371 | bytes 1516121 | solution.py:58
  648.7 7.7 collective-permute-done.8
  663.3 55.2 %all-reduce.11.cloned.1.call-done = bf16[32,4,256]{2,0,1:T(8,128)(2,1)} async-done(((bf16[32,4,256]{2,0,1:T(8,128)(2,1)}), bf16[32,4,256]{2,0,1:T(8,128)(2,1)}) %all-reduce.11.cloned.1.call-update) | async-done | bytes 65552 | tf_op jit(solution)/shard_map/psum | solution.py:108
  739.4 136.6 %while.293 = (s32[]{:T(128)}, bf16[32,1024]{1,0:T(8,128)(2,1)S(1)}, s32[8]{0:T(128)S(1)}, s32[8]{0:T(128)S(1)}, bf16[32,1024]{1,0:T(8,128)(2,1)S(1)}, /*index=5*...) while((s32[]{:T(128)}, bf16[32,1024]{1,0:T(8,128)(2,1)S(1)}, ...), condition=%wide.region_29.30_spmd, body=%wide.region_26.29_spmd.sunk | while | flops 11667697 | bytes 2303082 | solution.py:99
  754.5 10.4 collective-permute-start
  808.3 12.7 %while.301 = (s32[]{:T(128)}, f32[32,8,128]{2,1,0:T(8,128)S(1)}, s32[]{:T(128)}, s32[]{:T(128)}, s32[112]{0:T(128)S(1)}, /*index=5*/s32[]{:T(128)}, bf16[112,128...) while((s32[]{:T(128)}, f32[32,8,128]{2,1,0:T(8,128)S(1)}, ...), condition=%wide.region_28.28_spmd.clone.clone, body=%wide.region_27.27_spmd.clone.clone.sunk | while | flops 11569371 | bytes 1516121 | solution.py:58
  825.0 51.0 %while.301 = (s32[]{:T(128)}, f32[32,8,128]{2,1,0:T(8,128)S(1)}, s32[]{:T(128)}, s32[]{:T(128)}, s32[112]{0:T(128)S(1)}, /*index=5*/s32[]{:T(128)}, bf16[112,128...) while((s32[]{:T(128)}, f32[32,8,128]{2,1,0:T(8,128)S(1)}, ...), condition=%wide.region_28.28_spmd.clone.clone, body=%wide.region_27.27_spmd.clone.clone.sunk | while | flops 11569371 | bytes 1516121 | solution.py:58
  878.9 7.0 collective-permute-done.10
  892.8 321.2 %all-reduce.15.cloned.1.call-done = (f32[128,128]{1,0:T(8,128)}, f32[128,128]{1,0:T(8,128)}) async-done(((f32[128,128]{1,0:T(8,128)}, f32[128,128]{1,0:T(8,128)}), (f32[128,128]{1,0:T(8,128)}, f32[128,128]{1,0:T(8,128)})) %all-reduce.15.cloned.1.call-update) | async-done | bytes 131088 | tf_op jit(solution)/shard_map/psum | solution.py:118
  1215.5 49.2 %all-reduce.13.cloned.1.call-done = bf16[32,1024]{1,0:T(8,128)(2,1)} async-done(((bf16[32,1024]{1,0:T(8,128)(2,1)}), bf16[32,1024]{1,0:T(8,128)(2,1)}) %all-reduce.13.cloned.1.call-update) | async-done | bytes 65552 | tf_op jit(solution)/shard_map/psum | solution.py:147
  (977 shorter events, 764.6 us)
Async XLA Ops:
  7.2 236.6 %all-reduce.7.cloned.1.call-start = ((), (), s32[]{:S(2)}) async-start(), calls=%async_computation.6 | async-start | bytes 131072 | tf_op jit(solution)/shard_map/psum | solution.py:108
  7.2 15.6 %collective-permute-start.4 = (bf16[32,1024]{1,0:T(8,128)(2,1)}, bf16[32,1024]{1,0:T(8,128)(2,1)S(1)}, u32[]{:S(2)}, u32[]{:S(2)}) collective-permute-start(bf16[32,1024]{1,0:T(8,128)(2,1)} %param.31), channel_id=1, source_target_pairs={{0,16},{16,32},{32,48},{48,64},{64,80},{80,96},{96,112},{112,128},... | collective-permute-start | bytes 196616 | tf_op jit(solution)/shard_map/ppermute | solution.py:13
  103.7 9.1 collective-permute-start.3
  142.5 10.1 collective-permute-start.3
  189.3 300.8 %all-reduce.9.cloned.1.call-start = ((), (), s32[]{:S(2)}) async-start(), calls=%async_computation.7 | async-start | bytes 131072 | tf_op jit(solution)/shard_map/psum | solution.py:108
  256.8 9.8 collective-permute-start.6
  385.4 10.1 collective-permute-start.2
  502.5 216.1 %all-reduce.11.cloned.1.call-start = ((), (), s32[]{:S(2)}) async-start(), calls=%async_computation.8 | async-start | bytes 131072 | tf_op jit(solution)/shard_map/psum | solution.py:108
  511.3 15.0 %collective-permute-start.1 = (bf16[32,1024]{1,0:T(8,128)(2,1)S(1)}, bf16[32,1024]{1,0:T(8,128)(2,1)S(1)}, u32[]{:S(2)}, u32[]{:S(2)}) collective-permute-start(bf16[32,1024]{1,0:T(8,128)(2,1)S(1)} %get-tuple-element.3920), channel_id=1, source_target_pairs={{0,448},{16,464},{32,480},{48,496},{64,0},{80,16},{96,32},{112,48}... | collective-permute-start | bytes 196616 | tf_op jit(solution)/shard_map/while/body/eval_jaxpr/ppermute | solution.py:13
  526.4 18.7 %collective-permute-start.1 = (bf16[32,1024]{1,0:T(8,128)(2,1)S(1)}, bf16[32,1024]{1,0:T(8,128)(2,1)S(1)}, u32[]{:S(2)}, u32[]{:S(2)}) collective-permute-start(bf16[32,1024]{1,0:T(8,128)(2,1)S(1)} %get-tuple-element.3920), channel_id=1, source_target_pairs={{0,448},{16,464},{32,480},{48,496},{64,0},{80,16},{96,32},{112,48}... | collective-permute-start | bytes 196616 | tf_op jit(solution)/shard_map/while/body/eval_jaxpr/ppermute | solution.py:13
  552.2 13.4 %collective-permute-start.1 = (bf16[32,1024]{1,0:T(8,128)(2,1)S(1)}, bf16[32,1024]{1,0:T(8,128)(2,1)S(1)}, u32[]{:S(2)}, u32[]{:S(2)}) collective-permute-start(bf16[32,1024]{1,0:T(8,128)(2,1)S(1)} %get-tuple-element.3920), channel_id=1, source_target_pairs={{0,448},{16,464},{32,480},{48,496},{64,0},{80,16},{96,32},{112,48}... | collective-permute-start | bytes 196616 | tf_op jit(solution)/shard_map/while/body/eval_jaxpr/ppermute | solution.py:13
  565.6 10.2 collective-permute-start.1
  575.9 16.5 %collective-permute-start.1 = (bf16[32,1024]{1,0:T(8,128)(2,1)S(1)}, bf16[32,1024]{1,0:T(8,128)(2,1)S(1)}, u32[]{:S(2)}, u32[]{:S(2)}) collective-permute-start(bf16[32,1024]{1,0:T(8,128)(2,1)S(1)} %get-tuple-element.3920), channel_id=1, source_target_pairs={{0,448},{16,464},{32,480},{48,496},{64,0},{80,16},{96,32},{112,48}... | collective-permute-start | bytes 196616 | tf_op jit(solution)/shard_map/while/body/eval_jaxpr/ppermute | solution.py:13
  592.5 54.2 %collective-permute-start.1 = (bf16[32,1024]{1,0:T(8,128)(2,1)S(1)}, bf16[32,1024]{1,0:T(8,128)(2,1)S(1)}, u32[]{:S(2)}, u32[]{:S(2)}) collective-permute-start(bf16[32,1024]{1,0:T(8,128)(2,1)S(1)} %get-tuple-element.3920), channel_id=1, source_target_pairs={{0,448},{16,464},{32,480},{48,496},{64,0},{80,16},{96,32},{112,48}... | collective-permute-start | bytes 196616 | tf_op jit(solution)/shard_map/while/body/eval_jaxpr/ppermute | solution.py:13
  646.7 9.7 collective-permute-start.8
  730.6 483.4 %all-reduce.15.cloned.1.call-start = ((), (), s32[]{:S(2)}) async-start(), calls=%async_computation.10 | async-start | bytes 262144 | tf_op jit(solution)/shard_map/psum | solution.py:118
  739.4 15.1 %collective-permute-start = (bf16[32,1024]{1,0:T(8,128)(2,1)S(1)}, bf16[32,1024]{1,0:T(8,128)(2,1)S(1)}, u32[]{:S(2)}, u32[]{:S(2)}) collective-permute-start(bf16[32,1024]{1,0:T(8,128)(2,1)S(1)} %get-tuple-element.4004), channel_id=1, source_target_pairs={{0,448},{16,464},{32,480},{48,496},{64,0},{80,16},{96,32},{112,48}... | collective-permute-start | bytes 196616 | tf_op jit(solution)/shard_map/while/body/eval_jaxpr/ppermute | solution.py:13
  754.5 18.8 %collective-permute-start = (bf16[32,1024]{1,0:T(8,128)(2,1)S(1)}, bf16[32,1024]{1,0:T(8,128)(2,1)S(1)}, u32[]{:S(2)}, u32[]{:S(2)}) collective-permute-start(bf16[32,1024]{1,0:T(8,128)(2,1)S(1)} %get-tuple-element.4004), channel_id=1, source_target_pairs={{0,448},{16,464},{32,480},{48,496},{64,0},{80,16},{96,32},{112,48}... | collective-permute-start | bytes 196616 | tf_op jit(solution)/shard_map/while/body/eval_jaxpr/ppermute | solution.py:13
  780.5 13.5 %collective-permute-start = (bf16[32,1024]{1,0:T(8,128)(2,1)S(1)}, bf16[32,1024]{1,0:T(8,128)(2,1)S(1)}, u32[]{:S(2)}, u32[]{:S(2)}) collective-permute-start(bf16[32,1024]{1,0:T(8,128)(2,1)S(1)} %get-tuple-element.4004), channel_id=1, source_target_pairs={{0,448},{16,464},{32,480},{48,496},{64,0},{80,16},{96,32},{112,48}... | collective-permute-start | bytes 196616 | tf_op jit(solution)/shard_map/while/body/eval_jaxpr/ppermute | solution.py:13
  794.0 10.3 collective-permute-start
  804.4 16.6 %collective-permute-start = (bf16[32,1024]{1,0:T(8,128)(2,1)S(1)}, bf16[32,1024]{1,0:T(8,128)(2,1)S(1)}, u32[]{:S(2)}, u32[]{:S(2)}) collective-permute-start(bf16[32,1024]{1,0:T(8,128)(2,1)S(1)} %get-tuple-element.4004), channel_id=1, source_target_pairs={{0,448},{16,464},{32,480},{48,496},{64,0},{80,16},{96,32},{112,48}... | collective-permute-start | bytes 196616 | tf_op jit(solution)/shard_map/while/body/eval_jaxpr/ppermute | solution.py:13
  821.1 54.9 %collective-permute-start = (bf16[32,1024]{1,0:T(8,128)(2,1)S(1)}, bf16[32,1024]{1,0:T(8,128)(2,1)S(1)}, u32[]{:S(2)}, u32[]{:S(2)}) collective-permute-start(bf16[32,1024]{1,0:T(8,128)(2,1)S(1)} %get-tuple-element.4004), channel_id=1, source_target_pairs={{0,448},{16,464},{32,480},{48,496},{64,0},{80,16},{96,32},{112,48}... | collective-permute-start | bytes 196616 | tf_op jit(solution)/shard_map/while/body/eval_jaxpr/ppermute | solution.py:13
  876.0 9.9 collective-permute-start.10
  888.7 376.0 %all-reduce.13.cloned.1.call-start = ((), (), s32[]{:S(2)}) async-start(), calls=%async_computation.9 | async-start | bytes 131072 | tf_op jit(solution)/shard_map/psum | solution.py:147
  (23 other events, 785.2 us)
Sparse Core Ops, SparseCore 0:
  189.4 54.3 all-reduce.6
  432.4 57.7 all-reduce.8
  663.5 55.0 all-reduce.10
  888.8 325.1 all-reduce.14
  1216.1 48.5 all-reduce.12
where the time goes:
time: 1280 us; the launch traced here: 1270 us
  waiting for transfers between devices  650 us (51%)
  local copies, waits for them, and re-layouts  314 us (25%)
  starting transfers between devices  129 us (10%)
  other arithmetic  84 us (7%)
  matrix products  32.4 us (3%)
  loops' own time  25.1 us (2%)
  blocking collectives  23.3 us (2%)
  between operations  15.5 us (1%)
    psum x1, waiting for transfers between devices, weight_grad(): return lax.psum(part_sum, ('loop', 'feat'))  321 us
    psum x3, waiting for transfers between devices, to_nodes(): summed = lax.psum(partial_value.astype(jnp.bfloat16), 'rep')  168 us
    gather x60, local copies, waits for them, and re-layouts, one_round(): chosen = tile_set[slot_ids]  158 us
    ppermute x36, starting transfers between devices, passed_along(): return lax.ppermute(value, axis, pairs)  119 us
    ppermute x36, waiting for transfers between devices, passed_along(): return lax.ppermute(value, axis, pairs)  108 us
    psum x1, waiting for transfers between devices, shards(): input_grad = lax.psum(partial_value.astype(jnp.bfloat16), 'rep')  49.2 us
    lt x60, other arithmetic, one_round(): alive_mask = within < number  40 us
    gather x60, local copies, waits for them, and re-layouts, one_round(): picked = shaped[:, row_ids[slot_ids], :]  36.2 us
  transfers between devices with their start and end apart: 43, of which 31 were waited for; matrix products, arithmetic and copies ran while one was open for 17% of the time, Pallas kernels for 0%

commit v1 on v0

--- a/solution.py
+++ b/solution.py
@@ -5,6 +5,12 @@
 from jax.sharding import PartitionSpec as P
 
 tile_batch = 8
+
+
+def gather_and_add(array, axis):
+    terms = lax.all_gather(array, axis, axis=0, tiled=False)
+    acc = terms.sum(axis=0)
+    return acc
 
 
 def passed_along(value, axis, steps):
@@ -115,7 +121,7 @@
 
 def weight_grad(mixed, slope):
     part_sum = jnp.einsum("dq,eq->de", mixed, slope, preferred_element_type=jnp.float32)
-    return lax.psum(part_sum, ("loop", "feat"))
+    return gather_and_add(part_sum, ("loop", "feat"))
 
 
 def shards(features, tile_values, tile_coords, section_counts, weight_one, weight_two, cotangent):

time: 1280 us -> 1080 us (0.84)
  waiting for transfers between devices: 650 us -> 450 us
    psum x1 -> x0, waiting for transfers between devices: 321 us -> none  [weight_grad(): return lax.psum(part_sum, ('loop', 'feat'))]
    all_gather x0 -> x2, waiting for transfers between devices: none -> 118 us  [gather_and_add(): terms = lax.all_gather(array, axis, axis=0, tiled=False)]
  transfers between devices with their start and end apart: 43 -> 45, of which waited for: 31 -> 32; matrix products, arithmetic and copies ran while one was open for 17% -> 22% of each run, Pallas kernels for 0% -> 0%
where the time goes in v1:
time: 1080 us
  waiting for transfers between devices  450 us (42%)
  local copies, waits for them, and re-layouts  314 us (29%)
  starting transfers between devices  134 us (12%)
  other arithmetic  91.8 us (8%)
  matrix products  32.4 us (3%)
  loops' own time  24.1 us (2%)
  blocking collectives  17.2 us (2%)
  between operations  15.9 us (1%)
    psum x3, waiting for transfers between devices, to_nodes(): summed = lax.psum(partial_value.astype(jnp.bfloat16), 'rep')  167 us
    gather x60, local copies, waits for them, and re-layouts, one_round(): chosen = tile_set[slot_ids]  159 us
    ppermute x36, starting transfers between devices, passed_along(): return lax.ppermute(value, axis, pairs)  120 us
    all_gather x2, waiting for transfers between devices, gather_and_add(): terms = lax.all_gather(array, axis, axis=0, tiled=False)  118 us
    ppermute x36, waiting for transfers between devices, passed_along(): return lax.ppermute(value, axis, pairs)  110 us
    psum x1, waiting for transfers between devices, shards(): input_grad = lax.psum(partial_value.astype(jnp.bfloat16), 'rep')  50.3 us
    lt x60, other arithmetic, one_round(): alive_mask = within < number  39.3 us
    gather x60, local copies, waits for them, and re-layouts, one_round(): picked = shaped[:, row_ids[slot_ids], :]  36.2 us
  transfers between devices with their start and end apart: 45, of which 32 were waited for; matrix products, arithmetic and copies ran while one was open for 22% of the time, Pallas kernels for 0%

profile of v1, /device:TPU:8, one launch (start us, length us, event | category | flops | bytes accessed | tf_op | source)
XLA Modules:
  0.0 1079.1 jit_solution(16261774855965846544)
XLA Ops:
  15.8 7.0 collective-permute-done.4
  31.1 51.0 %while.294 = (s32[]{:T(128)}, f32[32,8,128]{2,1,0:T(8,128)S(1)}, s32[]{:T(128)}, s32[]{:T(128)}, s32[112]{0:T(128)S(1)}, /*index=5*/s32[]{:T(128)}, bf16[112,128...) while((s32[]{:T(128)}, f32[32,8,128]{2,1,0:T(8,128)S(1)}, ...), condition=%wide.region_2.3_spmd.clone.clone, body=%wide.region_1.2_spmd.clone.clone.sunk | while | flops 11569371 | bytes 1516121 | solution.py:64
  82.2 106.4 %while.287 = (s32[]{:T(128)}, bf16[32,1024]{1,0:T(8,128)(2,1)S(1)}, f32[32,1024]{1,0:T(8,128)S(1)}, s32[8]{0:T(128)S(1)}, s32[8]{0:T(128)S(1)}, /*index=5*/s32[1...) while((s32[]{:T(128)}, bf16[32,1024]{1,0:T(8,128)(2,1)S(1)}, ...), condition=%wide.region_6.7_spmd, body=%wide.region_3.6_spmd.sunk | while | flops 11602160 | bytes 2565222 | solution.py:89
  90.9 12.7 %while.298 = (s32[]{:T(128)}, f32[32,8,128]{2,1,0:T(8,128)S(1)}, s32[]{:T(128)}, s32[]{:T(128)}, s32[112]{0:T(128)S(1)}, /*index=5*/s32[]{:T(128)}, bf16[112,128...) while((s32[]{:T(128)}, f32[32,8,128]{2,1,0:T(8,128)S(1)}, ...), condition=%wide.region_5.5_spmd.clone.clone, body=%wide.region_4.4_spmd.clone.clone.sunk | while | flops 11569371 | bytes 1516121 | solution.py:64
  142.4 7.8 collective-permute-start.3
  189.3 54.5 %all-reduce.5.cloned.1.call-done = bf16[32,4,256]{2,1,0:T(4,128)(2,1)} async-done(((bf16[32,4,256]{2,1,0:T(4,128)(2,1)}), bf16[32,4,256]{2,1,0:T(4,128)(2,1)}) %all-reduce.5.cloned.1.call-update) | async-done | bytes 65552 | tf_op jit(solution)/shard_map/psum | solution.py:114
  274.0 51.0 %while.295 = (s32[]{:T(128)}, f32[32,8,128]{2,1,0:T(8,128)S(1)}, s32[]{:T(128)}, s32[]{:T(128)}, s32[112]{0:T(128)S(1)}, /*index=5*/s32[]{:T(128)}, bf16[112,128...) while((s32[]{:T(128)}, f32[32,8,128]{2,1,0:T(8,128)S(1)}, ...), condition=%wide.region_9.10_spmd.clone.clone, body=%wide.region_8.9_spmd.clone.clone.sunk | while | flops 11569371 | bytes 1516121 | solution.py:64
  325.1 107.0 %while.289 = (s32[]{:T(128)}, bf16[32,1024]{1,0:T(8,128)(2,1)S(1)}, f32[32,1024]{1,0:T(8,128)S(1)}, s32[8]{0:T(128)S(1)}, s32[8]{0:T(128)S(1)}, /*index=5*/s32[1...) while((s32[]{:T(128)}, bf16[32,1024]{1,0:T(8,128)(2,1)S(1)}, ...), condition=%wide.region_13.14_spmd, body=%wide.region_10.13_spmd.sunk | while | flops 11602160 | bytes 2565222 | solution.py:89
  334.1 12.9 %while.299 = (s32[]{:T(128)}, f32[32,8,128]{2,1,0:T(8,128)S(1)}, s32[]{:T(128)}, s32[]{:T(128)}, s32[112]{0:T(128)S(1)}, /*index=5*/s32[]{:T(128)}, bf16[112,128...) while((s32[]{:T(128)}, f32[32,8,128]{2,1,0:T(8,128)S(1)}, ...), condition=%wide.region_12.12_spmd.clone.clone, body=%wide.region_11.11_spmd.clone.clone.sunk | while | flops 11569371 | bytes 1516121 | solution.py:64
  385.8 7.0 collective-permute-start.2
  432.9 58.0 %all-reduce.7.cloned.1.call-done = bf16[32,4,256]{2,1,0:T(4,128)(2,1)} async-done(((bf16[32,4,256]{2,1,0:T(4,128)(2,1)}), bf16[32,4,256]{2,1,0:T(4,128)(2,1)}) %all-reduce.7.cloned.1.call-update) | async-done | bytes 65552 | tf_op jit(solution)/shard_map/psum | solution.py:114
  512.0 136.5 %while.291 = (s32[]{:T(128)}, bf16[32,1024]{1,0:T(8,128)(2,1)S(1)}, s32[8]{0:T(128)S(1)}, s32[8]{0:T(128)S(1)}, bf16[32,1024]{1,0:T(8,128)(2,1)S(1)}, /*index=5*...) while((s32[]{:T(128)}, bf16[32,1024]{1,0:T(8,128)(2,1)S(1)}, ...), condition=%wide.region_20.21_spmd, body=%wide.region_17.20_spmd.sunk | while | flops 11667697 | bytes 2303082 | solution.py:105
  527.1 10.4 collective-permute-start.1
  580.8 12.7 %while.300 = (s32[]{:T(128)}, f32[32,8,128]{2,1,0:T(8,128)S(1)}, s32[]{:T(128)}, s32[]{:T(128)}, s32[112]{0:T(128)S(1)}, /*index=5*/s32[]{:T(128)}, bf16[112,128...) while((s32[]{:T(128)}, f32[32,8,128]{2,1,0:T(8,128)S(1)}, ...), condition=%wide.region_19.19_spmd.clone.clone, body=%wide.region_18.18_spmd.clone.clone.sunk | while | flops 11569371 | bytes 1516121 | solution.py:64
  597.5 50.9 %while.300 = (s32[]{:T(128)}, f32[32,8,128]{2,1,0:T(8,128)S(1)}, s32[]{:T(128)}, s32[]{:T(128)}, s32[112]{0:T(128)S(1)}, /*index=5*/s32[]{:T(128)}, bf16[112,128...) while((s32[]{:T(128)}, f32[32,8,128]{2,1,0:T(8,128)S(1)}, ...), condition=%wide.region_19.19_spmd.clone.clone, body=%wide.region_18.18_spmd.clone.clone.sunk | while | flops 11569371 | bytes 1516121 | solution.py:64
  650.4 7.8 collective-permute-done.8
  665.9 54.3 %all-reduce.9.cloned.1.call-done = bf16[32,4,256]{2,0,1:T(8,128)(2,1)} async-done(((bf16[32,4,256]{2,0,1:T(8,128)(2,1)}), bf16[32,4,256]{2,0,1:T(8,128)(2,1)}) %all-reduce.9.cloned.1.call-update) | async-done | bytes 65552 | tf_op jit(solution)/shard_map/psum | solution.py:114
  741.0 135.8 %while.293 = (s32[]{:T(128)}, bf16[32,1024]{1,0:T(8,128)(2,1)S(1)}, s32[8]{0:T(128)S(1)}, s32[8]{0:T(128)S(1)}, bf16[32,1024]{1,0:T(8,128)(2,1)S(1)}, /*index=5*...) while((s32[]{:T(128)}, bf16[32,1024]{1,0:T(8,128)(2,1)S(1)}, ...), condition=%wide.region_29.30_spmd, body=%wide.region_26.29_spmd.sunk | while | flops 11667697 | bytes 2303082 | solution.py:105
  756.1 10.4 collective-permute-start
  809.6 12.6 %while.301 = (s32[]{:T(128)}, f32[32,8,128]{2,1,0:T(8,128)S(1)}, s32[]{:T(128)}, s32[]{:T(128)}, s32[112]{0:T(128)S(1)}, /*index=5*/s32[]{:T(128)}, bf16[112,128...) while((s32[]{:T(128)}, f32[32,8,128]{2,1,0:T(8,128)S(1)}, ...), condition=%wide.region_28.28_spmd.clone.clone, body=%wide.region_27.27_spmd.clone.clone.sunk | while | flops 11569371 | bytes 1516121 | solution.py:64
  826.2 50.6 %while.301 = (s32[]{:T(128)}, f32[32,8,128]{2,1,0:T(8,128)S(1)}, s32[]{:T(128)}, s32[]{:T(128)}, s32[112]{0:T(128)S(1)}, /*index=5*/s32[]{:T(128)}, bf16[112,128...) while((s32[]{:T(128)}, f32[32,8,128]{2,1,0:T(8,128)S(1)}, ...), condition=%wide.region_28.28_spmd.clone.clone, body=%wide.region_27.27_spmd.clone.clone.sunk | while | flops 11569371 | bytes 1516121 | solution.py:64
  879.2 7.8 collective-permute-done.10
  898.5 117.6 %all-gather.5.cloned.1.call-done = f32[16384,128]{1,0:T(8,128)} async-done(((f32[128,128]{1,0:T(8,128)}), f32[16384,128]{1,0:T(8,128)}) %all-gather.5.cloned.1.call-update) | async-done | bytes 8388624 | tf_op jit(solution)/shard_map/all_gather | solution.py:11
  1020.5 50.3 %all-reduce.11.cloned.1.call-done = bf16[32,1024]{1,0:T(8,128)(2,1)} async-done(((bf16[32,1024]{1,0:T(8,128)(2,1)}), bf16[32,1024]{1,0:T(8,128)(2,1)}) %all-reduce.11.cloned.1.call-update) | async-done | bytes 65552 | tf_op jit(solution)/shard_map/psum | solution.py:153
  (984 shorter events, 773.5 us)
Async XLA Ops:
  7.2 236.6 %all-reduce.5.cloned.1.call-start = ((), (), s32[]{:S(2)}) async-start(), calls=%async_computation.6 | async-start | bytes 131072 | tf_op jit(solution)/shard_map/psum | solution.py:114
  7.2 15.6 %collective-permute-start.4 = (bf16[32,1024]{1,0:T(8,128)(2,1)}, bf16[32,1024]{1,0:T(8,128)(2,1)S(1)}, u32[]{:S(2)}, u32[]{:S(2)}) collective-permute-start(bf16[32,1024]{1,0:T(8,128)(2,1)} %param.31), channel_id=1, source_target_pairs={{0,16},{16,32},{32,48},{48,64},{64,80},{80,96},{96,112},{112,128},... | collective-permute-start | bytes 196616 | tf_op jit(solution)/shard_map/ppermute | solution.py:19
  142.4 10.2 collective-permute-start.3
  189.3 301.6 %all-reduce.7.cloned.1.call-start = ((), (), s32[]{:S(2)}) async-start(), calls=%async_computation.7 | async-start | bytes 131072 | tf_op jit(solution)/shard_map/psum | solution.py:114
  256.8 9.8 collective-permute-start.6
  385.8 10.2 collective-permute-start.2
  503.2 217.1 %all-reduce.9.cloned.1.call-start = ((), (), s32[]{:S(2)}) async-start(), calls=%async_computation.8 | async-start | bytes 131072 | tf_op jit(solution)/shard_map/psum | solution.py:114
  512.0 15.1 %collective-permute-start.1 = (bf16[32,1024]{1,0:T(8,128)(2,1)S(1)}, bf16[32,1024]{1,0:T(8,128)(2,1)S(1)}, u32[]{:S(2)}, u32[]{:S(2)}) collective-permute-start(bf16[32,1024]{1,0:T(8,128)(2,1)S(1)} %get-tuple-element.3916), channel_id=1, source_target_pairs={{0,448},{16,464},{32,480},{48,496},{64,0},{80,16},{96,32},{112,48}... | collective-permute-start | bytes 196616 | tf_op jit(solution)/shard_map/while/body/eval_jaxpr/ppermute | solution.py:19
  527.1 18.7 %collective-permute-start.1 = (bf16[32,1024]{1,0:T(8,128)(2,1)S(1)}, bf16[32,1024]{1,0:T(8,128)(2,1)S(1)}, u32[]{:S(2)}, u32[]{:S(2)}) collective-permute-start(bf16[32,1024]{1,0:T(8,128)(2,1)S(1)} %get-tuple-element.3916), channel_id=1, source_target_pairs={{0,448},{16,464},{32,480},{48,496},{64,0},{80,16},{96,32},{112,48}... | collective-permute-start | bytes 196616 | tf_op jit(solution)/shard_map/while/body/eval_jaxpr/ppermute | solution.py:19
  553.0 13.5 %collective-permute-start.1 = (bf16[32,1024]{1,0:T(8,128)(2,1)S(1)}, bf16[32,1024]{1,0:T(8,128)(2,1)S(1)}, u32[]{:S(2)}, u32[]{:S(2)}) collective-permute-start(bf16[32,1024]{1,0:T(8,128)(2,1)S(1)} %get-tuple-element.3916), channel_id=1, source_target_pairs={{0,448},{16,464},{32,480},{48,496},{64,0},{80,16},{96,32},{112,48}... | collective-permute-start | bytes 196616 | tf_op jit(solution)/shard_map/while/body/eval_jaxpr/ppermute | solution.py:19
  566.6 10.3 collective-permute-start.1
  576.9 16.6 %collective-permute-start.1 = (bf16[32,1024]{1,0:T(8,128)(2,1)S(1)}, bf16[32,1024]{1,0:T(8,128)(2,1)S(1)}, u32[]{:S(2)}, u32[]{:S(2)}) collective-permute-start(bf16[32,1024]{1,0:T(8,128)(2,1)S(1)} %get-tuple-element.3916), channel_id=1, source_target_pairs={{0,448},{16,464},{32,480},{48,496},{64,0},{80,16},{96,32},{112,48}... | collective-permute-start | bytes 196616 | tf_op jit(solution)/shard_map/while/body/eval_jaxpr/ppermute | solution.py:19
  593.6 54.8 %collective-permute-start.1 = (bf16[32,1024]{1,0:T(8,128)(2,1)S(1)}, bf16[32,1024]{1,0:T(8,128)(2,1)S(1)}, u32[]{:S(2)}, u32[]{:S(2)}) collective-permute-start(bf16[32,1024]{1,0:T(8,128)(2,1)S(1)} %get-tuple-element.3916), channel_id=1, source_target_pairs={{0,448},{16,464},{32,480},{48,496},{64,0},{80,16},{96,32},{112,48}... | collective-permute-start | bytes 196616 | tf_op jit(solution)/shard_map/while/body/eval_jaxpr/ppermute | solution.py:19
  648.5 9.7 collective-permute-start.8
  665.1 228.9 %all-gather.7.cloned.1.call-start = ((), (), s32[]{:S(2)}) async-start(), calls=%async_computation.11 | async-start | bytes 8454144 | tf_op jit(solution)/shard_map/all_gather | solution.py:11
  732.3 283.8 %all-gather.5.cloned.1.call-start = ((), (), s32[]{:S(2)}) async-start(), calls=%async_computation.10 | async-start | bytes 8454144 | tf_op jit(solution)/shard_map/all_gather | solution.py:11
  733.1 337.7 %all-reduce.11.cloned.1.call-start = ((), (), s32[]{:S(2)}) async-start(), calls=%async_computation.9 | async-start | bytes 131072 | tf_op jit(solution)/shard_map/psum | solution.py:153
  741.0 15.0 %collective-permute-start = (bf16[32,1024]{1,0:T(8,128)(2,1)S(1)}, bf16[32,1024]{1,0:T(8,128)(2,1)S(1)}, u32[]{:S(2)}, u32[]{:S(2)}) collective-permute-start(bf16[32,1024]{1,0:T(8,128)(2,1)S(1)} %get-tuple-element.4000), channel_id=1, source_target_pairs={{0,448},{16,464},{32,480},{48,496},{64,0},{80,16},{96,32},{112,48}... | collective-permute-start | bytes 196616 | tf_op jit(solution)/shard_map/while/body/eval_jaxpr/ppermute | solution.py:19
  756.1 18.7 %collective-permute-start = (bf16[32,1024]{1,0:T(8,128)(2,1)S(1)}, bf16[32,1024]{1,0:T(8,128)(2,1)S(1)}, u32[]{:S(2)}, u32[]{:S(2)}) collective-permute-start(bf16[32,1024]{1,0:T(8,128)(2,1)S(1)} %get-tuple-element.4000), channel_id=1, source_target_pairs={{0,448},{16,464},{32,480},{48,496},{64,0},{80,16},{96,32},{112,48}... | collective-permute-start | bytes 196616 | tf_op jit(solution)/shard_map/while/body/eval_jaxpr/ppermute | solution.py:19
  782.1 13.3 %collective-permute-start = (bf16[32,1024]{1,0:T(8,128)(2,1)S(1)}, bf16[32,1024]{1,0:T(8,128)(2,1)S(1)}, u32[]{:S(2)}, u32[]{:S(2)}) collective-permute-start(bf16[32,1024]{1,0:T(8,128)(2,1)S(1)} %get-tuple-element.4000), channel_id=1, source_target_pairs={{0,448},{16,464},{32,480},{48,496},{64,0},{80,16},{96,32},{112,48}... | collective-permute-start | bytes 196616 | tf_op jit(solution)/shard_map/while/body/eval_jaxpr/ppermute | solution.py:19
  795.4 10.2 collective-permute-start
  805.7 16.5 %collective-permute-start = (bf16[32,1024]{1,0:T(8,128)(2,1)S(1)}, bf16[32,1024]{1,0:T(8,128)(2,1)S(1)}, u32[]{:S(2)}, u32[]{:S(2)}) collective-permute-start(bf16[32,1024]{1,0:T(8,128)(2,1)S(1)} %get-tuple-element.4000), channel_id=1, source_target_pairs={{0,448},{16,464},{32,480},{48,496},{64,0},{80,16},{96,32},{112,48}... | collective-permute-start | bytes 196616 | tf_op jit(solution)/shard_map/while/body/eval_jaxpr/ppermute | solution.py:19
  822.3 54.5 %collective-permute-start = (bf16[32,1024]{1,0:T(8,128)(2,1)S(1)}, bf16[32,1024]{1,0:T(8,128)(2,1)S(1)}, u32[]{:S(2)}, u32[]{:S(2)}) collective-permute-start(bf16[32,1024]{1,0:T(8,128)(2,1)S(1)} %get-tuple-element.4000), channel_id=1, source_target_pairs={{0,448},{16,464},{32,480},{48,496},{64,0},{80,16},{96,32},{112,48}... | collective-permute-start | bytes 196616 | tf_op jit(solution)/shard_map/while/body/eval_jaxpr/ppermute | solution.py:19
  876.9 10.2 collective-permute-start.10
  (25 other events, 801.8 us)
Sparse Core Ops, SparseCore 0:
  189.4 54.3 all-reduce.4
  433.0 57.7 all-reduce.6
  665.2 55.0 all-reduce.8
  723.8 145.8 all-gather.6
  873.3 142.7 all-gather.4
  1018.2 52.5 all-reduce.10
